TPU v7x, 32 devices: a whole 2x2x4 slice. The times are simulated.
32 devices in a mesh: clip: 8 (over y, x, core), tm: 4 (over z).
Axes of the slice: x: 2, y: 2, z: 4, core: 2. Of those that a mesh axis runs over, the one named last changes fastest.
Arguments:
- latent: bfloat16 [8, 32, 8, 32, 16], P('clip', 'tm'), may hold values from -6 to 6
- offsets: int32 [8], P('clip'), may hold values from 0 to 16
- teacher: bfloat16 [8, 32, 8, 16, 384], P('clip', 'tm'), may hold values from -6 to 6
- w_in: bfloat16 [432, 384], replicated, may hold values from -0.3125 to 0.3125
- w_mid: bfloat16 [10368, 384], P('clip'), may hold values from -0.0625 to 0.0625
Outputs:
- grad_mid: float32 [10368, 384], P('clip')
- grad_in: float32 [432, 384], replicated
Inputs may be any that keep to these rules, and one draw needn't show every extreme that they name: `offsets`: each clip's crop start among the latent columns.
All inputs are finite; a program needn't handle non-finite values.
Results may differ from a plain program's by a relative error of at most 0.00095.
Values may be sent and summed in bfloat16 or wider, within the bound.
No kernel may reach another device: no remote copies, remote signals or barrier semaphores. Data moves between devices by JAX's collectives and lax.ppermute only.
A program may use at most 192 MiB of HBM per device.

v0:
```python
import math
import jax
import jax.numpy as jnp
from jax import lax
from jax.sharding import PartitionSpec as P


def passed_along(block, axis, distance):
    devices = range(lax.axis_size(axis))
    route = [(i - distance, i) for i in devices if i - distance in devices]
    return lax.ppermute(block, axis, route)


def tap_masks(count, rows, cols):
    place = jnp.arange(count, dtype=jnp.int32) % (rows * cols)
    row_pos = place // cols
    col_pos = place % cols
    masks = []
    for row_off in range(3):
        for col_off in range(3):
            good_row = (row_pos + row_off - 1 >= 0) & (row_pos + row_off - 1 < rows)
            good_col = (col_pos + col_off - 1 >= 0) & (col_pos + col_off - 1 < cols)
            masks.append((good_row & good_col).astype(jnp.bfloat16).reshape(count, 1))
    return masks


def tap_slices(extended, count, rows, cols, masks):
    margin = jnp.zeros((cols + 1, extended.shape[1]), extended.dtype)
    padded = jnp.concatenate([margin, extended, margin], axis=0)
    plane = rows * cols
    pieces = []
    for depth in range(3):
        for row_off in range(3):
            for col_off in range(3):
                first = depth * plane + row_off * cols + col_off
                pieces.append(padded[first : first + count] * masks[row_off * 3 + col_off])
    return pieces


def cross_dot(left, right):
    return lax.dot_general(
        left, right, (((0,), (0,)), ((), ())), preferred_element_type=jnp.float32
    )


def shards(latent, offsets, teacher, w_in, w_mid):
    frames = teacher.shape[1]
    rows = teacher.shape[2]
    cols = teacher.shape[3]
    chans = teacher.shape[4]
    plane = rows * cols
    count = frames * plane
    lat_chans = latent.shape[4]
    total_cells = lax.axis_size("clip") * lax.axis_size("tm") * count
    scale = 2.0 / math.sqrt(total_cells)
    masks = tap_masks(count, rows, cols)
    crop = lax.dynamic_slice_in_dim(latent[0], offsets[0], cols, axis=2).reshape(count, lat_chans)
    earlier = passed_along(crop[count - 2 * plane :], "tm", 1)
    crop_ext = jnp.concatenate([earlier, crop], axis=0)
    patch_in = jnp.concatenate(tap_slices(crop_ext, count, rows, cols, masks), axis=1)
    z_first = jnp.dot(patch_in, w_in, preferred_element_type=jnp.float32)
    act = jax.nn.silu(z_first).astype(jnp.bfloat16)
    act_prev = passed_along(act[count - 2 * plane :], "tm", 1)
    act_ext = jnp.concatenate([act_prev, act], axis=0)
    act_taps = tap_slices(act_ext, count, rows, cols, masks)
    w_full = lax.all_gather(w_mid, "clip", axis=0, tiled=True)
    output = jnp.zeros((count, chans), jnp.float32)
    for k in range(27):
        output = output + jnp.dot(
            act_taps[k], w_full[k * chans : (k + 1) * chans], preferred_element_type=jnp.float32
        )
    target_rows = teacher[0].reshape(count, chans).astype(jnp.float32)
    grad_low = ((output - target_rows) * scale).astype(jnp.bfloat16)
    local_mid = jnp.concatenate([cross_dot(act_taps[k], grad_low) for k in range(27)], axis=0)
    lead = 2 * plane + cols + 1
    masked_pads = []
    for k in range(9):
        masked_pads.append(jnp.pad(grad_low * masks[k], ((lead, lead), (0, 0))))
    ext_count = count + 2 * plane
    adjoint = jnp.zeros((ext_count, chans), jnp.float32)
    for depth in range(3):
        for row_off in range(3):
            for col_off in range(3):
                k = depth * 9 + row_off * 3 + col_off
                first = (2 - depth) * plane + (2 - row_off) * cols + (2 - col_off)
                piece = masked_pads[row_off * 3 + col_off][first : first + ext_count]
                adjoint = adjoint + lax.dot_general(
                    piece,
                    w_full[k * chans : (k + 1) * chans],
                    (((1,), (1,)), ((), ())),
                    preferred_element_type=jnp.float32,
                )
    outgoing = adjoint[: 2 * plane]
    incoming = passed_along(outgoing.astype(jnp.bfloat16), "tm", -1).astype(outgoing.dtype)
    own = adjoint[2 * plane :]
    dact = jnp.concatenate([own[: count - 2 * plane], own[count - 2 * plane :] + incoming], axis=0)
    sig = jax.nn.sigmoid(z_first)
    dz_first = (dact * sig * (1.0 + z_first * (1.0 - sig))).astype(jnp.bfloat16)
    grad_in = lax.psum(cross_dot(patch_in, dz_first), ("clip", "tm"))
    summed = lax.psum(local_mid, "tm")
    grad_mid = lax.psum_scatter(summed, "clip", scatter_dimension=0, tiled=True)
    return (grad_mid, grad_in)


def solution(mesh):
    return jax.shard_map(
        shards,
        mesh=mesh,
        in_specs=(
            P("clip", "tm", None, None, None),
            P("clip"),
            P("clip", "tm", None, None, None),
            P(),
            P("clip", None),
        ),
        out_specs=(P("clip", None), P()),
        check_vma=False,
    )
```

profile of v0, /device:TPU:0, one launch (start us, length us, event | category | flops | bytes accessed | tf_op | source)
XLA Modules:
  0.0 524.9 jit_solution(12850490637867089896)
XLA Ops:
  9.7 4.9 collective-permute-start
  18.5 2.0 multiply_convert_fusion
  20.5 3.9 collective-permute-start.1
  24.4 3.4 collective-permute-done.1
  27.8 2.3 concatenate.47
  30.2 35.1 %all-gather.2.cloned.1.call-done = bf16[10368,384]{1,0:T(8,128)(2,1)} async-done(((bf16[1296,384]{1,0:T(8,128)(2,1)}), bf16[10368,384]{1,0:T(8,128)(2,1)}) %all-gather.2.cloned.1.call-update) | async-done | bytes 7962640 | tf_op jit(solution)/shard_map/all_gather | solution.py:66
  65.3 3.0 fusion.52
  68.3 2.8 fusion.51
  71.1 2.8 fusion.50
  73.9 1.9 fusion.49
  75.8 1.9 fusion.132
  77.7 1.9 fusion.129
  79.5 1.9 fusion.126
  81.4 1.9 fusion.123
  83.3 1.8 fusion.120
  85.2 1.8 fusion.117
  87.0 1.9 fusion.114
  88.9 1.9 fusion.111
  90.7 1.9 fusion.108
  92.7 1.8 fusion.105
  94.5 1.9 fusion.102
  96.4 2.0 fusion.99
  98.4 1.9 fusion.96
  100.2 2.1 fusion.93
  102.3 1.9 fusion.90
  104.2 1.9 fusion.87
  106.1 1.9 fusion.84
  108.0 1.9 fusion.46
  109.9 1.9 fusion.47
  111.8 1.9 fusion.48
  113.7 1.9 fusion.45
  115.6 1.8 fusion.43
  117.4 17.8 %broadcast_multiply_fusion = (bf16[1024,384]{1,0:T(8,128)(2,1)S(1)}, bf16[1024,384]{1,0:T(8,128)(2,1)S(1)}, bf16[1024,384]{1,0:T(8,128)(2,1)S(1)}, bf16[1024,384...) fusion(bf16[1024]{0:T(1024)(128)(2,1)S(1)} %get-tuple-element.1, ...), kind=kOutput, calls=%fused_computation.165 | convolution fusion | flops 319684608 | bytes 50843648 | tf_op jit(solution)/shard_map/dot_general | solution.py:69
  135.3 3.1 convolution_dynamic-update-slice_fusion.26
  138.4 1.6 convolution_dynamic-update-slice_fusion.25
  144.9 1.6 convolution_dynamic-update-slice_fusion.21
  146.5 1.6 convolution_dynamic-update-slice_fusion.20
  148.2 1.6 convolution_dynamic-update-slice_fusion.19
  149.8 1.7 convolution_dynamic-update-slice_fusion.18
  151.5 1.6 convolution_dynamic-update-slice_fusion.17
  153.1 1.6 convolution_dynamic-update-slice_fusion.16
  154.7 1.6 convolution_dynamic-update-slice_fusion.15
  156.4 1.7 convolution_dynamic-update-slice_fusion.14
  158.0 1.7 convolution_dynamic-update-slice_fusion.13
  159.7 1.7 convolution_dynamic-update-slice_fusion.12
  161.4 1.6 convolution_dynamic-update-slice_fusion.11
  164.6 1.7 convolution_dynamic-update-slice_fusion.9
  166.3 1.6 convolution_dynamic-update-slice_fusion.8
  169.6 1.6 convolution_dynamic-update-slice_fusion.6
  171.2 1.9 convolution_dynamic-update-slice_fusion.5
  174.7 1.6 convolution_dynamic-update-slice_fusion.3
  176.4 1.6 convolution_dynamic-update-slice_fusion.2
  178.0 1.6 convolution_dynamic-update-slice_fusion.1
  179.6 1.7 convolution_dynamic-update-slice_fusion
  181.4 2.0 fusion.4
  183.5 1.9 convolution_add_fusion.25
  185.4 1.9 convolution_add_fusion.24
  187.3 1.9 convolution_add_fusion.23
  210.1 7.5 %collective-permute-done.2 = bf16[256,384]{1,0:T(8,128)(2,1)S(1)} collective-permute-done((bf16[256,384]{1,0:T(8,128)(2,1)S(1)}, bf16[256,384]{1,0:T(8,128)(2,1)S(1)}, u32[]{:S(2)}, u32[]{:S(2)}) %collective-permute-start.2) | collective-permute-done | bytes 196640 | tf_op jit(solution)/shard_map/ppermute | solution.py:11
  217.7 1.8 fusion.40
  219.6 74.8 %reduce-scatter.2.cloned.1.call-done = f32[1296,384]{1,0:T(8,128)} async-done(((f32[10368,384]{1,0:T(8,128)}), f32[1296,384]{1,0:T(8,128)}) %reduce-scatter.2.cloned.1.call-update) | async-done | bytes 1990672 | tf_op jit(solution)/shard_map/reduce_scatter | solution.py:101
  294.4 133.7 %all-reduce.14.cloned.1.call-done = f32[432,384]{1,0:T(8,128)} async-done(((f32[432,384]{1,0:T(8,128)}), f32[432,384]{1,0:T(8,128)}) %all-reduce.14.cloned.1.call-update) | async-done | bytes 663568 | tf_op jit(solution)/shard_map/psum | solution.py:99
  428.1 86.2 %all-reduce.16.cloned.1.call-done = f32[1296,384]{1,0:T(8,128)} async-done(((f32[1296,384]{1,0:T(8,128)}), f32[1296,384]{1,0:T(8,128)}) %all-reduce.16.cloned.1.call-update) | async-done | bytes 1990672 | tf_op jit(solution)/shard_map/psum | solution.py:100
  514.3 3.0 copy.65
  (125 shorter events, 37.0 us)
Async XLA Ops:
  7.2 11.3 %copy-start = (bf16[432,384]{1,0:T(8,128)(2,1)S(1)}, bf16[432,384]{1,0:T(8,128)(2,1)}, u32[]{:S(2)}) copy-start(bf16[432,384]{1,0:T(8,128)(2,1)} %param.8) | copy-start | bytes 995332
  7.2 58.1 %all-gather.2.cloned.1.call-start = ((), (), s32[]{:S(2)}) async-start(), calls=%async_computation.1 | async-start | bytes 8957952 | tf_op jit(solution)/shard_map/all_gather | solution.py:66
  7.9 286.4 %reduce-scatter.2.cloned.1.call-start = ((), (), s32[]{:S(2)}) async-start(), calls=%async_computation.3 | async-start | bytes 17915904 | tf_op jit(solution)/shard_map/reduce_scatter | solution.py:101
  9.7 6.6 %collective-permute-start = (bf16[256,16]{0,1:T(8,128)(2,1)S(1)}, bf16[256,16]{0,1:T(8,128)(2,1)S(1)}, u32[]{:S(2)}, u32[]{:S(2)}) collective-permute-start(bf16[256,16]{0,1:T(8,128)(2,1)S(1)} %slice.384), channel_id=1, source_target_pairs={{0,1},{1,2},{2,3},{4,5},{5,6},{6,7},{8,9},{9,10},{10,11},{12,13},{... | collective-permute-start | bytes 24584 | tf_op jit(solution)/shard_map/ppermute | solution.py:11
  18.5 2.0 copy-start.13
  20.5 7.4 %collective-permute-start.1 = (bf16[256,384]{1,0:T(8,128)(2,1)S(1)}, bf16[256,384]{1,0:T(8,128)(2,1)S(1)}, u32[]{:S(2)}, u32[]{:S(2)}) collective-permute-start(bf16[256,384]{1,0:T(8,128)(2,1)S(1)} %slice.517), channel_id=1, source_target_pairs={{0,1},{1,2},{2,3},{4,5},{5,6},{6,7},{8,9},{9,10},{10,11},{12,13},{... | collective-permute-start | bytes 589832 | tf_op jit(solution)/shard_map/ppermute | solution.py:11
  30.2 43.8 %copy-start.9 = (bf16[1297,384]{1,0:T(8,128)(2,1)}, bf16[1297,384]{1,0:T(8,128)(2,1)S(1)}, u32[]{:S(2)}) copy-start(bf16[1297,384]{1,0:T(8,128)(2,1)S(1)} %concatenate.47) | copy-start | bytes 2988292
  65.3 8.7 %copy-start.2 = (bf16[10368,384]{1,0:T(8,128)(2,1)S(1)}, bf16[10368,384]{1,0:T(8,128)(2,1)}, u32[]{:S(2)}) copy-start(bf16[10368,384]{1,0:T(8,128)(2,1)} %all-gather.2.cloned.1.call-done) | copy-start | bytes 23887876
  135.3 3.1 copy-start.10
  135.3 3.1 copy-start.11
  181.3 2.1 copy-start.7
  181.3 246.8 %all-reduce.14.cloned.1.call-start = ((), (), s32[]{:S(2)}) async-start(), calls=%async_computation.2 | async-start | bytes 1327104 | tf_op jit(solution)/shard_map/psum | solution.py:99
  183.4 1.9 copy-start.6
  183.4 5.7 %slice-start = ((s8[7962624]{0:T(1024)(128)(4,1)}), s8[4194304]{0:T(1024)(128)(4,1)S(1)}, s32[]{:S(2)}) async-start(s8[7962624]{0:T(1024)(128)(4,1)} %bitcast.44), calls=%async_computation.5 | async-start | bytes 8388608
  185.4 1.9 copy-start.5
  185.4 3.8 slice-start.1
  187.3 1.9 copy-start.4
  189.2 1.3 copy-start.3
  192.8 1.3 copy-start.8
  208.5 9.2 %copy-start.14 = (bf16[1024,432]{0,1:T(8,128)(2,1)S(1)}, bf16[1024,432]{0,1:T(8,128)(2,1)}, u32[]{:S(2)}) copy-start(bf16[1024,432]{0,1:T(8,128)(2,1)} %copy-done.13) | copy-start | bytes 2654212
  208.5 9.2 %copy-start.15 = (f32[1024,384]{1,0:T(8,128)S(1)}, f32[1024,384]{1,0:T(8,128)}, u32[]{:S(2)}) copy-start(f32[1024,384]{1,0:T(8,128)} %get-tuple-element.12) | copy-start | bytes 4718596
  208.5 9.2 %collective-permute-start.2 = (bf16[256,384]{1,0:T(8,128)(2,1)S(1)}, bf16[256,384]{1,0:T(8,128)(2,1)S(1)}, u32[]{:S(2)}, u32[]{:S(2)}) collective-permute-start(bf16[256,384]{1,0:T(8,128)(2,1)S(1)} %slice.1014), channel_id=1, source_target_pairs={{1,0},{2,1},{3,2},{5,4},{6,5},{7,6},{9,8},{10,9},{11,10},{13,12},{... | collective-permute-start | bytes 589832 | tf_op jit(solution)/shard_map/ppermute | solution.py:11
  219.5 294.8 %all-reduce.16.cloned.1.call-start = ((), (), s32[]{:S(2)}) async-start(), calls=%async_computation.4 | async-start | bytes 3981312 | tf_op jit(solution)/shard_map/psum | solution.py:100
  428.1 89.2 %copy-start.12 = (f32[432,384]{1,0:T(8,128)S(1)}, f32[432,384]{1,0:T(8,128)}, u32[]{:S(2)}) copy-start(f32[432,384]{1,0:T(8,128)} %all-reduce.14.cloned.1.call-done) | copy-start | bytes 1990660
  514.3 3.9 copy-start.1
Sparse Core Ops, SparseCore 0:
  9.9 55.3 all-gather.1
  181.4 112.8 reduce-scatter.1
  301.0 127.0 all-reduce.13
  430.4 83.9 all-reduce.15
where the time goes:
time: 528 us; the launch traced here: 525 us
  waiting for transfers between devices  342 us (65%)
  matrix products  145 us (27%)
  between operations  15.4 us (3%)
  starting transfers between devices  10.6 us (2%)
  local copies, waits for them, and re-layouts  10 us (2%)
    psum x1, waiting for transfers between devices, shards(): grad_in = lax.psum(cross_dot(patch_in, dz_first), ('clip', 'tm'))  134 us
    psum x1, waiting for transfers between devices, shards(): summed = lax.psum(local_mid, 'tm')  86.2 us
    reduce_scatter x1, waiting for transfers between devices, shards(): grad_mid = lax.psum_scatter(summed, 'clip', scatter_dimension=0, tiled=True)  74.8 us
    dot_general x27, matrix products, shards(): jnp.dot(act_taps[k], w_full[k * chans:(k + 1) * chans], preferred_element...  70 us
    dot_general x28, matrix products, cross_dot(): lax.dot_general(left, right, (((0,), (0,)), ((), ())), preferred_element_...  47.7 us
    all_gather x1, waiting for transfers between devices, shards(): w_full = lax.all_gather(w_mid, 'clip', axis=0, tiled=True)  35.1 us
    dot_general x27, matrix products, shards(): lax.dot_general(piece, w_full[k * chans:(k + 1) * chans], (((1,), (1,)),...  25.7 us
    ppermute x3, waiting for transfers between devices, passed_along(): return lax.ppermute(block, axis, route)  11 us
  transfers between devices with their start and end apart: 7, of which 6 were waited for; matrix products, arithmetic and copies ran while one was open for 7% of the time, Pallas kernels for 0%

commit v1 on v0

--- a/solution.py
+++ b/solution.py
@@ -96,7 +96,8 @@
     dact = jnp.concatenate([own[: count - 2 * plane], own[count - 2 * plane :] + incoming], axis=0)
     sig = jax.nn.sigmoid(z_first)
     dz_first = (dact * sig * (1.0 + z_first * (1.0 - sig))).astype(jnp.bfloat16)
-    grad_in = lax.psum(cross_dot(patch_in, dz_first), ("clip", "tm"))
+    inner = lax.psum(cross_dot(patch_in, dz_first), "tm")
+    grad_in = lax.psum(inner, "clip")
     summed = lax.psum(local_mid, "tm")
     grad_mid = lax.psum_scatter(summed, "clip", scatter_dimension=0, tiled=True)
     return (grad_mid, grad_in)

time: 528 us -> 473 us (0.90)
  waiting for transfers between devices: 342 us -> 287 us
    psum x1, waiting for transfers between devices: 134 us -> 56.7 us  [shards(): grad_in = lax.psum(inner, 'clip')]
    psum x1, waiting for transfers between devices: 86.2 us -> 109 us  [shards(): summed = lax.psum(local_mid, 'tm')]
  transfers between devices with their start and end apart: 7 -> 7, of which waited for: 6 -> 6; matrix products, arithmetic and copies ran while one was open for 7% -> 8% of each run, Pallas kernels for 0% -> 0%
where the time goes in v1:
time: 473 us; the launch traced here: 470 us
  waiting for transfers between devices  287 us (61%)
  matrix products  145 us (31%)
  between operations  15.4 us (3%)
  starting transfers between devices  10.6 us (2%)
  local copies, waits for them, and re-layouts  10 us (2%)
    psum x1, waiting for transfers between devices, shards(): summed = lax.psum(local_mid, 'tm')  109 us
    reduce_scatter x1, waiting for transfers between devices, shards(): grad_mid = lax.psum_scatter(summed, 'clip', scatter_dimension=0, tiled=True)  74.9 us
    dot_general x27, matrix products, shards(): jnp.dot(act_taps[k], w_full[k * chans:(k + 1) * chans], preferred_element...  69.9 us
    psum x1, waiting for transfers between devices, shards(): grad_in = lax.psum(inner, 'clip')  56.7 us
    dot_general x28, matrix products, cross_dot(): lax.dot_general(left, right, (((0,), (0,)), ((), ())), preferred_element_...  47.7 us
    all_gather x1, waiting for transfers between devices, shards(): w_full = lax.all_gather(w_mid, 'clip', axis=0, tiled=True)  35.1 us
    dot_general x27, matrix products, shards(): lax.dot_general(piece, w_full[k * chans:(k + 1) * chans], (((1,), (1,)),...  25.7 us
    ppermute x3, waiting for transfers between devices, passed_along(): return lax.ppermute(block, axis, route)  11 us
  transfers between devices with their start and end apart: 7, of which 6 were waited for; matrix products, arithmetic and copies ran while one was open for 8% of the time, Pallas kernels for 0%

profile of v1, /device:TPU:0, one launch (start us, length us, event | category | flops | bytes accessed | tf_op | source)
XLA Modules:
  0.0 470.3 jit_solution(15622604135744062736)
XLA Ops:
  9.7 4.9 %collective-permute-start = (bf16[256,16]{0,1:T(8,128)(2,1)S(1)}, bf16[256,16]{0,1:T(8,128)(2,1)S(1)}, u32[]{:S(2)}, u32[]{:S(2)}) collective-permute-start(bf16[256,16]{0,1:T(8,128)(2,1)S(1)} %slice.384), channel_id=1, source_target_pairs={{0,1},{1,2},{2,3},{4,5},{5,6},{6,7},{8,9},{9,10},{10,11},{12,13},{... | collective-permute-start | bytes 24584 | tf_op jit(solution)/shard_map/ppermute | solution.py:11
  18.5 2.0 multiply_convert_fusion
  20.5 3.9 collective-permute-start.1
  24.4 3.4 collective-permute-done.1
  27.8 2.3 concatenate.47
  30.2 35.1 %all-gather.2.cloned.1.call-done = bf16[10368,384]{1,0:T(8,128)(2,1)} async-done(((bf16[1296,384]{1,0:T(8,128)(2,1)}), bf16[10368,384]{1,0:T(8,128)(2,1)}) %all-gather.2.cloned.1.call-update) | async-done | bytes 7962640 | tf_op jit(solution)/shard_map/all_gather | solution.py:66
  65.3 3.0 fusion.52
  68.3 2.8 fusion.51
  71.1 2.8 fusion.50
  73.9 1.9 fusion.49
  75.8 1.9 fusion.132
  77.6 1.8 fusion.129
  79.5 1.8 fusion.126
  81.3 1.9 fusion.123
  83.3 1.8 fusion.120
  85.1 1.8 fusion.117
  86.9 1.9 fusion.114
  88.8 1.9 fusion.111
  90.7 1.9 fusion.108
  92.6 1.8 fusion.105
  94.5 1.9 fusion.102
  96.3 1.9 fusion.99
  98.3 1.9 fusion.96
  100.2 2.1 fusion.93
  102.2 1.9 fusion.90
  104.1 1.9 fusion.87
  106.0 1.9 fusion.84
  107.9 1.9 fusion.46
  109.8 1.8 fusion.47
  111.7 1.9 fusion.48
  113.6 1.9 fusion.45
  115.5 1.8 fusion.43
  117.3 17.8 %broadcast_multiply_fusion = (bf16[1024,384]{1,0:T(8,128)(2,1)S(1)}, bf16[1024,384]{1,0:T(8,128)(2,1)S(1)}, bf16[1024,384]{1,0:T(8,128)(2,1)S(1)}, bf16[1024,384...) fusion(bf16[1024]{0:T(1024)(128)(2,1)S(1)} %get-tuple-element.1, ...), kind=kOutput, calls=%fused_computation.165 | convolution fusion | flops 319684608 | bytes 50843648 | tf_op jit(solution)/shard_map/dot_general | solution.py:69
  135.2 3.1 convolution_dynamic-update-slice_fusion.26
  138.3 1.7 convolution_dynamic-update-slice_fusion.25
  140.0 1.6 convolution_dynamic-update-slice_fusion.24
  141.6 1.6 convolution_dynamic-update-slice_fusion.23
  144.8 1.6 convolution_dynamic-update-slice_fusion.21
  146.5 1.6 convolution_dynamic-update-slice_fusion.20
  148.1 1.6 convolution_dynamic-update-slice_fusion.19
  149.7 1.6 convolution_dynamic-update-slice_fusion.18
  151.4 1.6 convolution_dynamic-update-slice_fusion.17
  154.6 1.6 convolution_dynamic-update-slice_fusion.15
  156.2 1.7 convolution_dynamic-update-slice_fusion.14
  157.9 1.7 convolution_dynamic-update-slice_fusion.13
  159.6 1.7 convolution_dynamic-update-slice_fusion.12
  161.3 1.6 convolution_dynamic-update-slice_fusion.11
  164.5 1.7 convolution_dynamic-update-slice_fusion.9
  166.2 1.6 convolution_dynamic-update-slice_fusion.8
  167.8 1.6 convolution_dynamic-update-slice_fusion.7
  169.5 1.6 convolution_dynamic-update-slice_fusion.6
  171.1 1.9 convolution_dynamic-update-slice_fusion.5
  176.2 1.6 convolution_dynamic-update-slice_fusion.2
  179.5 1.7 convolution_dynamic-update-slice_fusion
  181.2 2.0 fusion.4
  183.3 1.9 convolution_add_fusion.25
  185.2 1.9 convolution_add_fusion.24
  187.1 1.9 convolution_add_fusion.23
  210.0 7.5 %collective-permute-done.2 = bf16[256,384]{1,0:T(8,128)(2,1)S(1)} collective-permute-done((bf16[256,384]{1,0:T(8,128)(2,1)S(1)}, bf16[256,384]{1,0:T(8,128)(2,1)S(1)}, u32[]{:S(2)}, u32[]{:S(2)}) %collective-permute-start.2) | collective-permute-done | bytes 196640 | tf_op jit(solution)/shard_map/ppermute | solution.py:11
  217.6 1.8 fusion.40
  219.3 74.9 %reduce-scatter.2.cloned.1.call-done = f32[1296,384]{1,0:T(8,128)} async-done(((f32[10368,384]{1,0:T(8,128)}), f32[1296,384]{1,0:T(8,128)}) %reduce-scatter.2.cloned.1.call-update) | async-done | bytes 1990672 | tf_op jit(solution)/shard_map/reduce_scatter | solution.py:102
  294.3 108.6 %all-reduce.17.cloned.1.call-done = (f32[1296,384]{1,0:T(8,128)}, f32[432,384]{1,0:T(8,128)}) async-done(((f32[1296,384]{1,0:T(8,128)}, f32[432,384]{1,0:T(8,128)}), (f32[1296,384]{1,0:T(8,128)}, f32[432,384]{1,0:T(8,128)})) %all-reduce.17.cloned.1.call-update) | async-done | bytes 2654224 | tf_op jit(solution)/shard_map/psum | solution.py:101
  403.0 56.7 %all-reduce.15.cloned.1.call-done = f32[432,384]{1,0:T(8,128)} async-done(((f32[432,384]{1,0:T(8,128)}), f32[432,384]{1,0:T(8,128)}) %all-reduce.15.cloned.1.call-update) | async-done | bytes 663568 | tf_op jit(solution)/shard_map/psum | solution.py:100
  459.7 3.0 copy.66
  (125 shorter events, 36.9 us)
Async XLA Ops:
  7.2 11.3 %copy-start = (bf16[432,384]{1,0:T(8,128)(2,1)S(1)}, bf16[432,384]{1,0:T(8,128)(2,1)}, u32[]{:S(2)}) copy-start(bf16[432,384]{1,0:T(8,128)(2,1)} %param.8) | copy-start | bytes 995332
  7.2 58.1 %all-gather.2.cloned.1.call-start = ((), (), s32[]{:S(2)}) async-start(), calls=%async_computation.1 | async-start | bytes 8957952 | tf_op jit(solution)/shard_map/all_gather | solution.py:66
  7.9 286.3 %reduce-scatter.2.cloned.1.call-start = ((), (), s32[]{:S(2)}) async-start(), calls=%async_computation.3 | async-start | bytes 17915904 | tf_op jit(solution)/shard_map/reduce_scatter | solution.py:102
  9.7 6.6 %collective-permute-start = (bf16[256,16]{0,1:T(8,128)(2,1)S(1)}, bf16[256,16]{0,1:T(8,128)(2,1)S(1)}, u32[]{:S(2)}, u32[]{:S(2)}) collective-permute-start(bf16[256,16]{0,1:T(8,128)(2,1)S(1)} %slice.384), channel_id=1, source_target_pairs={{0,1},{1,2},{2,3},{4,5},{5,6},{6,7},{8,9},{9,10},{10,11},{12,13},{... | collective-permute-start | bytes 24584 | tf_op jit(solution)/shard_map/ppermute | solution.py:11
  18.5 2.0 copy-start.13
  20.5 7.4 %collective-permute-start.1 = (bf16[256,384]{1,0:T(8,128)(2,1)S(1)}, bf16[256,384]{1,0:T(8,128)(2,1)S(1)}, u32[]{:S(2)}, u32[]{:S(2)}) collective-permute-start(bf16[256,384]{1,0:T(8,128)(2,1)S(1)} %slice.517), channel_id=1, source_target_pairs={{0,1},{1,2},{2,3},{4,5},{5,6},{6,7},{8,9},{9,10},{10,11},{12,13},{... | collective-permute-start | bytes 589832 | tf_op jit(solution)/shard_map/ppermute | solution.py:11
  30.2 43.7 %copy-start.9 = (bf16[1297,384]{1,0:T(8,128)(2,1)}, bf16[1297,384]{1,0:T(8,128)(2,1)S(1)}, u32[]{:S(2)}) copy-start(bf16[1297,384]{1,0:T(8,128)(2,1)S(1)} %concatenate.47) | copy-start | bytes 2988292
  65.3 8.6 %copy-start.2 = (bf16[10368,384]{1,0:T(8,128)(2,1)S(1)}, bf16[10368,384]{1,0:T(8,128)(2,1)}, u32[]{:S(2)}) copy-start(bf16[10368,384]{1,0:T(8,128)(2,1)} %all-gather.2.cloned.1.call-done) | copy-start | bytes 23887876
  135.2 3.1 copy-start.10
  135.2 3.1 copy-start.11
  181.2 2.1 copy-start.7
  181.2 221.7 %all-reduce.17.cloned.1.call-start = ((), (), s32[]{:S(2)}) async-start(), calls=%async_computation.4 | async-start | bytes 5308416 | tf_op jit(solution)/shard_map/psum | solution.py:101
  183.3 1.9 copy-start.6
  183.3 5.7 %slice-start = ((s8[7962624]{0:T(1024)(128)(4,1)}), s8[4194304]{0:T(1024)(128)(4,1)S(1)}, s32[]{:S(2)}) async-start(s8[7962624]{0:T(1024)(128)(4,1)} %bitcast.44), calls=%async_computation.5 | async-start | bytes 8388608
  185.2 1.9 copy-start.5
  185.2 3.8 slice-start.1
  187.1 1.9 copy-start.4
  189.1 1.3 copy-start.3
  192.7 1.3 copy-start.8
  208.3 9.3 %copy-start.14 = (bf16[1024,432]{0,1:T(8,128)(2,1)S(1)}, bf16[1024,432]{0,1:T(8,128)(2,1)}, u32[]{:S(2)}) copy-start(bf16[1024,432]{0,1:T(8,128)(2,1)} %copy-done.13) | copy-start | bytes 2654212
  208.3 9.3 %copy-start.15 = (f32[1024,384]{1,0:T(8,128)S(1)}, f32[1024,384]{1,0:T(8,128)}, u32[]{:S(2)}) copy-start(f32[1024,384]{1,0:T(8,128)} %get-tuple-element.14) | copy-start | bytes 4718596
  208.3 9.2 %collective-permute-start.2 = (bf16[256,384]{1,0:T(8,128)(2,1)S(1)}, bf16[256,384]{1,0:T(8,128)(2,1)S(1)}, u32[]{:S(2)}, u32[]{:S(2)}) collective-permute-start(bf16[256,384]{1,0:T(8,128)(2,1)S(1)} %slice.1014), channel_id=1, source_target_pairs={{1,0},{2,1},{3,2},{5,4},{6,5},{7,6},{9,8},{10,9},{11,10},{13,12},{... | collective-permute-start | bytes 589832 | tf_op jit(solution)/shard_map/ppermute | solution.py:11
  294.2 165.4 %all-reduce.15.cloned.1.call-start = ((), (), s32[]{:S(2)}) async-start(), calls=%async_computation.2 | async-start | bytes 1327104 | tf_op jit(solution)/shard_map/psum | solution.py:100
  459.7 3.1 copy-start.12
  459.7 3.9 copy-start.1
Sparse Core Ops, SparseCore 0:
  9.9 55.3 all-gather.1
  181.3 112.8 reduce-scatter.1
  297.4 105.5 all-reduce.16
  406.3 53.3 all-reduce.14
